TPU v7x, 32 devices: a whole 2x2x4 slice. The times are simulated.
32 devices in a mesh: grp: 4 (over x, core), blk: 8 (over z, y).
Axes of the slice: x: 2, y: 2, z: 4, core: 2. Of those that a mesh axis runs over, the one named last changes fastest.
Arguments:
- vertices: float32 [3, 8192], P(None, ('grp', 'blk')), may hold values from -6 to 6
- faces: int32 [3, 16384], P(None, ('grp', 'blk')), may hold values from 0 to 255
- trial_step: float32 [3, 8192], P(None, ('grp', 'blk')), may hold values from -2 to 2
- accepted: int32 [4], P('grp'), may hold values from 0 to 1
- face_weight: float32 [16384], P(('grp', 'blk')), may hold values from 0.5 to 6
- partner_shift: int32 [2, 4], replicated, may hold values from 1 to 3, as said below
Outputs:
- vertex_grad: float32 [3, 8192], P(None, ('grp', 'blk'))
- energy: float32 [1], replicated
Inputs may be any that keep to these rules, and one draw needn't show every extreme that they name: `partner_shift`: for each group the 2 offsets are all different, and the first round's offset is 4 // 2 for every group.
All inputs are finite; a program needn't handle non-finite values.
Results may differ from a plain program's by a relative error of at most 0.0001.
Values sent between devices are 32-bit elements; how exact they have to be, the bound alone decides.
No kernel may reach another device: no remote copies, remote signals or barrier semaphores. Data moves between devices by JAX's collectives and lax.ppermute only.
A program may use at most 64 MiB of HBM per device.

v0:
```python
import jax
import jax.numpy as jnp
from jax import lax
from jax.sharding import PartitionSpec as P

HOPS = 4


EPS2 = 0.05


def from_behind(value, axis, by):
    count = lax.axis_size(axis)
    return lax.ppermute(value, axis, [(i, (i + by) % count) for i in range(count)])


def pair_energy(own_geo, own_weight, other_geo, other_weight):
    d0 = own_geo[0][:, None] - other_geo[0][None, :]
    d1 = own_geo[1][:, None] - other_geo[1][None, :]
    d2 = own_geo[2][:, None] - other_geo[2][None, :]
    dist = d0 * d0 + d1 * d1 + d2 * d2 + EPS2
    proj_own = own_geo[3][:, None] * d0 + own_geo[4][:, None] * d1 + own_geo[5][:, None] * d2
    proj_other = (
        other_geo[3][None, :] * d0 + other_geo[4][None, :] * d1 + other_geo[5][None, :] * d2
    )
    kernel = (
        own_weight[:, None]
        * other_weight[None, :]
        * (proj_own * proj_own + proj_other * proj_other)
        / (dist * dist)
    )
    return jnp.sum(kernel)


def tile(own, other):
    count = own.shape[1]
    rows = count // 2 if count >= 1024 else count

    def visit(index, carry):
        energy, grad_own, grad_other = carry
        start = index * rows
        piece = lax.dynamic_slice_in_dim(own, start, rows, 1)

        def energy_of(first, second):
            return pair_energy(first, piece[6], second, other[6])

        value, pullback = jax.vjp(energy_of, piece[:6], other[:6])
        part_own, part_other = pullback(jnp.ones_like(value))
        grad_own = lax.dynamic_update_slice_in_dim(grad_own, part_own, start, 1)
        return (energy + value, grad_own, grad_other + part_other)

    init = (
        jnp.zeros((), jnp.float32),
        jnp.zeros((6, count), jnp.float32),
        jnp.zeros((6, other.shape[1]), jnp.float32),
    )
    return lax.fori_loop(0, count // rows, visit, init)


def geometry(pos, faces):
    first = pos[:, faces[0]]
    second = pos[:, faces[1]]
    third = pos[:, faces[2]]
    center = (first + second + third) / 3.0
    normal = 0.5 * jnp.cross(second - first, third - first, axis=0)
    return jnp.concatenate([center, normal], 0)


def chain(own, moves, energy, grad):
    moving = own
    carried = jnp.zeros((6, own.shape[1]), jnp.float32)
    for offset in moves:
        moving, carried = from_behind((moving, carried), "blk", offset)
        value, grad_own, grad_other = tile(own, moving)
        energy = energy + value
        grad = grad + grad_own
        carried = carried + grad_other
    carried = from_behind(carried, "blk", -sum(moves))
    return (energy, grad + carried)


def shards(vertices, faces, trial_step, accepted, face_weight, partner_shift):
    count = faces.shape[1]
    pos = vertices + accepted[0].astype(jnp.float32) * trial_step

    def geo_of(p):
        return geometry(p, faces)

    geo, pull = jax.vjp(geo_of, pos)
    own = jnp.concatenate([geo, face_weight[None, :]], 0)
    value, grad_a, grad_b = tile(own, own)
    energy = 0.5 * value
    grad = 0.5 * (grad_a + grad_b)
    energy, grad = chain(own, [-1] * (HOPS // 2), energy, grad)
    energy, grad = chain(own, [HOPS // 2 + 1] + [1] * (HOPS - HOPS // 2 - 1), energy, grad)
    groups = lax.axis_size("grp")
    blocks = lax.all_gather(own[None], "grp", axis=0, tiled=True)
    group = lax.axis_index("grp")
    rounds = partner_shift.shape[0]
    slots = jnp.zeros((groups, 6, count), jnp.float32)
    for r in range(rounds):
        ahead = (group + partner_shift[r, group]) % groups
        value, grad_own, grad_other = tile(own, lax.dynamic_index_in_dim(blocks, ahead, 0, False))
        energy = energy + value
        grad = grad + grad_own
        chosen = (jnp.arange(groups) == ahead).astype(jnp.float32)
        slots = slots + chosen[:, None, None] * grad_other[None]
    returned = lax.psum_scatter(slots, "grp", scatter_dimension=0, tiled=True)
    grad = grad + returned[0]
    vertex_grad = pull(grad)[0] / count
    devices = groups * lax.axis_size("blk")
    total = lax.psum(energy, ("grp", "blk"))
    total = total / (count * count * devices)
    return (vertex_grad, total.reshape(1))


def solution(mesh):
    placed = (
        P(None, ("grp", "blk")),
        P(None, ("grp", "blk")),
        P(None, ("grp", "blk")),
        P("grp"),
        P(("grp", "blk")),
        P(),
    )
    return jax.shard_map(
        shards,
        mesh=mesh,
        in_specs=placed,
        out_specs=(P(None, ("grp", "blk")), P()),
        check_vma=False,
    )
```

profile of v0, /device:TPU:0, one launch (start us, length us, event | category | flops | bytes accessed | tf_op | source)
XLA Modules:
  0.0 132.3 jit_solution(5620914261309485540)
XLA Ops:
  7.2 0.0 reduce-scatter.2.cloned.1.call-start
  7.2 0.8 compare_select_fusion.1
  8.0 0.0 copy-start.2
  8.1 0.0 copy-start.1
  8.7 0.0 copy-done.2
  8.7 0.0 copy-done.1
  8.8 0.1 copy.334
  8.9 1.0 gather_fusion
  9.9 0.1 copy.335
  10.1 1.0 gather_fusion.1
  11.1 0.1 copy.337
  11.2 1.0 gather_fusion.2
  12.3 0.1 copy.339
  12.4 0.0 copy-start.3
  12.5 0.7 copy-done.3
  13.1 6.1 %collective-permute-start = (f32[7,512]{1,0:T(8,128)S(1)}, f32[7,512]{1,0:T(8,128)S(1)}, u32[]{:S(2)}, u32[]{:S(2)}) collective-permute-start(f32[7,512]{1,0:T(8,128)S(1)} %pad_maximum_fusion), channel_id=1, source_target_pairs={{0,7},{1,0},{2,1},{3,2},{4,3},{5,4},{6,5},{7,6},{8,15},{9,8},{10,9... | collective-permute-start | bytes 43016 | tf_op jit(solution)/shard_map/ppermute | solution.py:14
  19.2 0.0 collective-permute-start.5
  19.2 1.7 %collective-permute-start.2 = (f32[6,512]{1,0:T(8,128)S(1)}, f32[6,512]{1,0:T(8,128)S(1)}, u32[]{:S(2)}, u32[]{:S(2)}) collective-permute-start(f32[6,512]{1,0:T(8,128)S(1)} %broadcast.296), channel_id=1, source_target_pairs={{0,7},{1,0},{2,1},{3,2},{4,3},{5,4},{6,5},{7,6},{8,15},{9,8},{10,9... | collective-permute-start | bytes 36872 | tf_op jit(solution)/shard_map/ppermute | solution.py:14
  20.9 0.2 collective-permute-start.7
  21.2 0.0 copy-start.4
  21.2 0.7 copy-done.4
  21.9 0.6 constant_dynamic-slice_fusion.14
  23.8 5.2 %all-gather.1 = f32[4,7,512]{2,1,0:T(8,128)S(1)} all-gather(f32[1,7,512]{2,1,0:T(8,128)S(1)} %bitcast.231), channel_id=2, replica_groups=mesh['grp'=4,'blk'=8] {'grp'}, dimensions={0}, use_global_device_ids=true | all-gather | bytes 71680 | tf_op jit(solution)/shard_map/all_gather | solution.py:97
  29.1 4.2 %divide_reduce_fusion.1 = (f32[]{:T(128)}, f32[512]{0:T(512)S(1)}, f32[512]{0:T(512)S(1)}, f32[512]{0:T(512)S(1)}, f32[512]{0:T(512)S(1)}, /*index=5*/f32[512]{0...) fusion(f32[512]{0:T(512)S(1)} %bitcast.349, ...), kind=kLoop, calls=%fused_computation.315 | loop fusion | flops 19654656 | bytes 53252 | tf_op jit(solution)/shard_map/while/body/eval_jaxpr/jvp()/reduce_sum | solution.py:32
  33.2 8.0 %divide_reduce_fusion = (f32[]{:T(128)}, f32[512]{0:T(512)S(1)}, f32[512]{0:T(512)S(1)}, f32[512]{0:T(512)S(1)}, f32[512]{0:T(512)S(1)}, /*index=5*/f32[512]{0:T...) fusion(f32[512]{0:T(512)S(1)} %bitcast.336, ...), kind=kLoop, calls=%fused_computation.314 | loop fusion | flops 39309312 | bytes 77832 | tf_op jit(solution)/shard_map/while/body/eval_jaxpr/jvp()/reduce_sum | solution.py:32
  41.3 0.7 multiply_add_fusion
  42.0 0.0 reduce-scatter.2.cloned.1.call-update
  42.0 0.0 collective-permute-done
  42.1 4.2 %divide_reduce_fusion.5 = (f32[]{:T(128)}, f32[512]{0:T(512)S(1)}, f32[512]{0:T(512)S(1)}, f32[512]{0:T(512)S(1)}, f32[512]{0:T(512)S(1)}, /*index=5*/f32[512]{0...) fusion(f32[512]{0:T(512)S(1)} %bitcast.322, ...), kind=kLoop, calls=%fused_computation.319 | loop fusion | flops 19654656 | bytes 53252 | tf_op jit(solution)/shard_map/while/body/eval_jaxpr/jvp()/reduce_sum | solution.py:32
  46.2 0.0 collective-permute-done.2
  46.3 3.8 %collective-permute-start.3 = (f32[6,512]{1,0:T(8,128)S(1)}, f32[6,512]{1,0:T(8,128)S(1)}, u32[]{:S(2)}, u32[]{:S(2)}) collective-permute-start(f32[6,512]{1,0:T(8,128)S(1)} %add_add_fusion.24), channel_id=1, source_target_pairs={{0,7},{1,0},{2,1},{3,2},{4,3},{5,4},{6,5},{7,6},{8,15},{9,8},{10,9... | collective-permute-start | bytes 36872 | tf_op jit(solution)/shard_map/ppermute | solution.py:14
  50.0 0.0 collective-permute-done.5
  50.1 4.1 %divide_reduce_fusion.3 = (f32[]{:T(128)}, f32[512]{0:T(512)S(1)}, f32[512]{0:T(512)S(1)}, f32[512]{0:T(512)S(1)}, f32[512]{0:T(512)S(1)}, /*index=5*/f32[512]{0...) fusion(f32[512]{0:T(512)S(1)} %bitcast.329, ...), kind=kLoop, calls=%fused_computation.317 | loop fusion | flops 19654656 | bytes 53252 | tf_op jit(solution)/shard_map/while/body/eval_jaxpr/jvp()/reduce_sum | solution.py:32
  54.2 1.1 collective-permute-start.1
  55.3 0.0 collective-permute-done.7
  55.4 0.9 collective-permute-start.8
  56.3 0.1 collective-permute-start.6
  56.5 1.5 %collective-permute-done.1 = f32[7,512]{1,0:T(8,128)S(1)} collective-permute-done((f32[7,512]{1,0:T(8,128)S(1)}, f32[7,512]{1,0:T(8,128)S(1)}, u32[]{:S(2)}, u32[]{:S(2)}) %collective-permute-start.1) | collective-permute-done | bytes 14368 | tf_op jit(solution)/shard_map/ppermute | solution.py:14
  58.0 4.2 %divide_reduce_fusion.4 = (f32[]{:T(128)}, f32[512]{0:T(512)S(1)}, f32[512]{0:T(512)S(1)}, f32[512]{0:T(512)S(1)}, f32[512]{0:T(512)S(1)}, /*index=5*/f32[512]{0...) fusion(f32[512]{0:T(512)S(1)} %bitcast.315, ...), kind=kLoop, calls=%fused_computation.318 | loop fusion | flops 19654656 | bytes 53252 | tf_op jit(solution)/shard_map/while/body/eval_jaxpr/jvp()/reduce_sum | solution.py:32
  62.2 0.0 collective-permute-done.3
  62.2 1.0 collective-permute-start.4
  63.3 0.0 collective-permute-done.6
  63.3 4.3 %divide_reduce_fusion.2 = (f32[]{:T(128)}, f32[512]{0:T(512)S(1)}, f32[512]{0:T(512)S(1)}, f32[512]{0:T(512)S(1)}, f32[512]{0:T(512)S(1)}, /*index=5*/f32[512]{0...) fusion(f32[512]{0:T(512)S(1)} %bitcast.308, ...), kind=kLoop, calls=%fused_computation.316 | loop fusion | flops 19654656 | bytes 53252 | tf_op jit(solution)/shard_map/while/body/eval_jaxpr/jvp()/reduce_sum | solution.py:32
  67.6 0.0 collective-permute-done.8
  67.6 2.4 %collective-permute-start.9 = (f32[6,512]{1,0:T(8,128)S(1)}, f32[6,512]{1,0:T(8,128)S(1)}, u32[]{:S(2)}, u32[]{:S(2)}) collective-permute-start(f32[6,512]{1,0:T(8,128)S(1)} %add_add_fusion.21), channel_id=1, source_target_pairs={{0,4},{1,5},{2,6},{3,7},{4,0},{5,1},{6,2},{7,3},{8,12},{9,13},{10,... | collective-permute-start | bytes 36872 | tf_op jit(solution)/shard_map/ppermute | solution.py:14
  74.4 39.1 %psum.7 = f32[]{:T(128)} all-reduce(f32[]{:T(128)S(6)} %add.707), channel_id=1, replica_groups=mesh['grp'=4,'blk'=8] {'grp','blk'}, use_global_device_ids=true, to_apply=%region_95.0 | all-reduce | flops 1 | bytes 8 | tf_op jit(solution)/shard_map/psum | solution.py:112
  114.2 0.0 collective-permute-done.4
  114.2 0.0 collective-permute-done.9
  114.2 0.0 reduce-scatter.2.cloned.1.call-done
  114.2 0.0 copy-start
  114.2 0.7 copy-done
  114.9 0.1 bitcast_add_fusion
  115.1 0.1 copy.341
  115.3 2.3 %scatter_custom_fusion.1 = f32[3,256]{0,1:T(8,128)S(1)} fusion(s32[512]{0:T(512)S(1)} %bitcast.258, f32[512,3]{1,0:T(8,128)S(1)} %copy.341, f32[]{:T(128)} %constant.111.clone.1), kind=kCustom, calls=%fused_computation.336 | custom fusion | flops 1536 | bytes 3076 | tf_op jit(solution)/shard_map/transpose(jvp())/scatter-add | solution.py:62
  117.6 0.1 copy.340
  117.7 2.3 %scatter_custom_fusion = f32[3,256]{0,1:T(8,128)S(1)} fusion(s32[512]{0:T(512)S(1)} %bitcast.256, f32[512,3]{1,0:T(8,128)S(1)} %copy.340, f32[]{:T(128)} %constant.111.clone.1), kind=kCustom, calls=%fused_computation.338 | custom fusion | flops 1536 | bytes 3076 | tf_op jit(solution)/shard_map/transpose(jvp())/scatter-add | solution.py:63
  120.0 0.1 copy.342
  120.2 3.4 %scatter_fusion = f32[3,256]{0,1:T(8,128)S(1)} fusion(f32[3,256]{0,1:T(8,128)S(1)} %add_any.844, s32[512]{0:T(512)S(1)} %bitcast.233, f32[512,3]{1,0:T(8,128)S(1)} %copy.342), kind=kCustom, calls=%fused_computation.5 | custom fusion | flops 1536 | bytes 20480 | tf_op jit(solution)/shard_map/transpose(jvp())/scatter-add | solution.py:61
  123.6 0.7 copy.343
  (49 shorter events, 0.4 us)
Async XLA Ops:
  7.2 107.0 %reduce-scatter.2.cloned.1.call-start = ((), (), s32[]{:S(2)}) async-start(), calls=%async_computation.1 | async-start | bytes 81920 | tf_op jit(solution)/shard_map/reduce_scatter | solution.py:108
  8.0 0.7 copy-start.2
  8.1 0.7 copy-start.1
  12.4 0.7 copy-start.3
  13.1 28.9 %collective-permute-start = (f32[7,512]{1,0:T(8,128)S(1)}, f32[7,512]{1,0:T(8,128)S(1)}, u32[]{:S(2)}, u32[]{:S(2)}) collective-permute-start(f32[7,512]{1,0:T(8,128)S(1)} %pad_maximum_fusion), channel_id=1, source_target_pairs={{0,7},{1,0},{2,1},{3,2},{4,3},{5,4},{6,5},{7,6},{8,15},{9,8},{10,9... | collective-permute-start | bytes 43016 | tf_op jit(solution)/shard_map/ppermute | solution.py:14
  19.2 30.8 %collective-permute-start.5 = (f32[7,512]{1,0:T(8,128)S(1)}, f32[7,512]{1,0:T(8,128)S(1)}, u32[]{:S(2)}, u32[]{:S(2)}) collective-permute-start(f32[7,512]{1,0:T(8,128)S(1)} %pad_maximum_fusion), channel_id=1, source_target_pairs={{0,3},{1,4},{2,5},{3,6},{4,7},{5,0},{6,1},{7,2},{8,11},{9,12},{10,... | collective-permute-start | bytes 43016 | tf_op jit(solution)/shard_map/ppermute | solution.py:14
  19.2 27.0 %collective-permute-start.2 = (f32[6,512]{1,0:T(8,128)S(1)}, f32[6,512]{1,0:T(8,128)S(1)}, u32[]{:S(2)}, u32[]{:S(2)}) collective-permute-start(f32[6,512]{1,0:T(8,128)S(1)} %broadcast.296), channel_id=1, source_target_pairs={{0,7},{1,0},{2,1},{3,2},{4,3},{5,4},{6,5},{7,6},{8,15},{9,8},{10,9... | collective-permute-start | bytes 36872 | tf_op jit(solution)/shard_map/ppermute | solution.py:14
  20.9 34.4 %collective-permute-start.7 = (f32[6,512]{1,0:T(8,128)S(1)}, f32[6,512]{1,0:T(8,128)S(1)}, u32[]{:S(2)}, u32[]{:S(2)}) collective-permute-start(f32[6,512]{1,0:T(8,128)S(1)} %broadcast.296), channel_id=1, source_target_pairs={{0,3},{1,4},{2,5},{3,6},{4,7},{5,0},{6,1},{7,2},{8,11},{9,12},{10,... | collective-permute-start | bytes 36872 | tf_op jit(solution)/shard_map/ppermute | solution.py:14
  21.2 0.7 copy-start.4
  46.3 15.9 %collective-permute-start.3 = (f32[6,512]{1,0:T(8,128)S(1)}, f32[6,512]{1,0:T(8,128)S(1)}, u32[]{:S(2)}, u32[]{:S(2)}) collective-permute-start(f32[6,512]{1,0:T(8,128)S(1)} %add_add_fusion.24), channel_id=1, source_target_pairs={{0,7},{1,0},{2,1},{3,2},{4,3},{5,4},{6,5},{7,6},{8,15},{9,8},{10,9... | collective-permute-start | bytes 36872 | tf_op jit(solution)/shard_map/ppermute | solution.py:14
  54.2 3.7 %collective-permute-start.1 = (f32[7,512]{1,0:T(8,128)S(1)}, f32[7,512]{1,0:T(8,128)S(1)}, u32[]{:S(2)}, u32[]{:S(2)}) collective-permute-start(f32[7,512]{1,0:T(8,128)S(1)} %collective-permute-done), channel_id=1, source_target_pairs={{0,7},{1,0},{2,1},{3,2},{4,3},{5,4},{6,5},{7,6},{8,15},{9,8},{10,9... | collective-permute-start | bytes 43016 | tf_op jit(solution)/shard_map/ppermute | solution.py:14
  55.4 12.2 %collective-permute-start.8 = (f32[6,512]{1,0:T(8,128)S(1)}, f32[6,512]{1,0:T(8,128)S(1)}, u32[]{:S(2)}, u32[]{:S(2)}) collective-permute-start(f32[6,512]{1,0:T(8,128)S(1)} %add_add_fusion.22), channel_id=1, source_target_pairs={{0,1},{1,2},{2,3},{3,4},{4,5},{5,6},{6,7},{7,0},{8,9},{9,10},{10,1... | collective-permute-start | bytes 36872 | tf_op jit(solution)/shard_map/ppermute | solution.py:14
  56.3 7.0 %collective-permute-start.6 = (f32[7,512]{1,0:T(8,128)S(1)}, f32[7,512]{1,0:T(8,128)S(1)}, u32[]{:S(2)}, u32[]{:S(2)}) collective-permute-start(f32[7,512]{1,0:T(8,128)S(1)} %collective-permute-done.5), channel_id=1, source_target_pairs={{0,1},{1,2},{2,3},{3,4},{4,5},{5,6},{6,7},{7,0},{8,9},{9,10},{10,1... | collective-permute-start | bytes 43016 | tf_op jit(solution)/shard_map/ppermute | solution.py:14
  62.2 51.9 %collective-permute-start.4 = (f32[6,512]{1,0:T(8,128)S(1)}, f32[6,512]{1,0:T(8,128)S(1)}, u32[]{:S(2)}, u32[]{:S(2)}) collective-permute-start(f32[6,512]{1,0:T(8,128)S(1)} %add_add_fusion.23), channel_id=1, source_target_pairs={{0,2},{1,3},{2,4},{3,5},{4,6},{5,7},{6,0},{7,1},{8,10},{9,11},{10,... | collective-permute-start | bytes 36872 | tf_op jit(solution)/shard_map/ppermute | solution.py:14
  67.6 46.6 %collective-permute-start.9 = (f32[6,512]{1,0:T(8,128)S(1)}, f32[6,512]{1,0:T(8,128)S(1)}, u32[]{:S(2)}, u32[]{:S(2)}) collective-permute-start(f32[6,512]{1,0:T(8,128)S(1)} %add_add_fusion.21), channel_id=1, source_target_pairs={{0,4},{1,5},{2,6},{3,7},{4,0},{5,1},{6,2},{7,3},{8,12},{9,13},{10,... | collective-permute-start | bytes 36872 | tf_op jit(solution)/shard_map/ppermute | solution.py:14
  114.2 0.7 copy-start
Sparse Core Ops, SparseCore 0:
  42.2 21.0 reduce-scatter.1
where the time goes:
time: 133 us; the launch traced here: 132 us
  blocking collectives  44.3 us (33%)
  other arithmetic  38.9 us (29%)
  between operations  22.6 us (17%)
  starting transfers between devices  17.5 us (13%)
  local copies, waits for them, and re-layouts  7.44 us (6%)
  waiting for transfers between devices  1.55 us (1%)
    psum x1, blocking collectives, shards(): total = lax.psum(energy, ('grp', 'blk'))  39.1 us
    reduce_sum x6, other arithmetic, pair_energy(): return jnp.sum(kernel)  29 us
    ppermute x10, starting transfers between devices, from_behind(): lax.ppermute(value, axis, [(i, (i + by) % count) for i in range(count)])  17.4 us
    all_gather x1, blocking collectives, shards(): blocks = lax.all_gather(own[None], 'grp', axis=0, tiled=True)  5.24 us
    scatter-add x1, other arithmetic, geometry(): first = pos[:, faces[0]]  3.37 us
    unnamed x11, local copies, waits for them, and re-layouts  2.75 us
  transfers between devices with their start and end apart: 11, of which 1 were waited for; matrix products, arithmetic and copies ran while one was open for 23% of the time, Pallas kernels for 0%

commit v1 on v0

v1 whole, which is shorter than its diff:
```python
import functools

import jax
import jax.numpy as jnp
from jax import lax
from jax.experimental import pallas as pl
from jax.experimental.pallas import tpu as pltpu
from jax.sharding import PartitionSpec as P

HOPS = 4
EPS2 = 0.05
ROWS = 8
LANES = 128
F32 = jnp.float32
BF16 = jnp.bfloat16
VMEM = pl.BlockSpec(memory_space=pltpu.VMEM)
SMEM = pl.BlockSpec(memory_space=pltpu.SMEM)


def flip(value, axis, mask):
    count = lax.axis_size(axis)
    return lax.ppermute(value, axis, [(i, i ^ mask) for i in range(count)])


def from_ahead(value, axis, by):
    count = lax.axis_size(axis)
    return lax.ppermute(value, axis, [(i, (i - by) % count) for i in range(count)])


def pieces(value):
    high = value.astype(BF16)
    rest = value - high.astype(F32)
    middle = rest.astype(BF16)
    low = (rest - middle.astype(F32)).astype(BF16)
    return high, middle, low


def one_hot(row, count):
    rows = lax.broadcasted_iota(jnp.int32, (count, row.shape[1]), 0)
    return jnp.where(rows == row, 1.0, 0.0).astype(BF16)


def geometry_kernel(accepted, vertices, trial_step, faces, weight, own, edges, padded):
    verts = vertices.shape[1]
    count = faces.shape[1]
    padded[...] = jnp.zeros_like(padded)
    padded[0:3, :] = vertices[...] + accepted[0].astype(F32) * trial_step[...]
    left = jnp.concatenate(pieces(padded[...]), 0)

    def corner(k):
        picked = jnp.dot(left, one_hot(faces[k : k + 1, :], verts), preferred_element_type=F32)
        picked = picked[0:ROWS] + picked[ROWS : 2 * ROWS] + picked[2 * ROWS : 3 * ROWS]
        return [picked[c : c + 1] for c in range(3)]

    first, second, third = corner(0), corner(1), corner(2)
    for c in range(3):
        own[c : c + 1, :] = (first[c] + second[c] + third[c]) / 3.0
    e1 = [second[c] - first[c] for c in range(3)]
    e2 = [third[c] - first[c] for c in range(3)]
    for c in range(3):
        n, m = (c + 1) % 3, (c + 2) % 3
        own[3 + c : 4 + c, :] = 0.5 * (e1[n] * e2[m] - e1[m] * e2[n])
        edges[c : c + 1, :] = e1[c]
        edges[3 + c : 4 + c, :] = e2[c]
    own[6:7, :] = weight[...].reshape(1, count)
    own[7:8, :] = jnp.zeros((1, count), F32)
    edges[6:8, :] = jnp.zeros((2, count), F32)


def window_times(offset, blocks):
    times = 0
    for k in range(1, HOPS + 1):
        times += ((k - offset) % blocks == 0).astype(jnp.int32) if not isinstance(offset, int) else int((k - offset) % blocks == 0)
        times += ((k + offset) % blocks == 0).astype(jnp.int32) if not isinstance(offset, int) else int((k + offset) % blocks == 0)
    return times


def partner_times(shift, here, there, groups):
    times = jnp.int32(0)
    for r in range(shift.shape[0]):
        times += (lax.rem(here + shift[r, here], groups) == there).astype(jnp.int32)
        times += (lax.rem(there + shift[r, there], groups) == here).astype(jnp.int32)
    return times


def multiplicity(kind, shift, groups, blocks):
    name, value = kind
    if name == "self":
        return 1.0 + window_times(0, blocks)
    if name == "blk":
        return float(window_times(value, blocks))
    if name == "blk^":
        here = lax.axis_index("blk")
        there = here ^ value
        return window_times(lax.rem(there - here + blocks, blocks), blocks).astype(F32)
    here = lax.axis_index("grp")
    there = here ^ value if name == "grp^" else lax.rem(here + value, groups)
    return partner_times(shift, here, there, groups).astype(F32)


def tiles_kernel(plan, groups, blocks, carry, adds, *refs):
    shift, own = refs[0], refs[1]
    count = own.shape[1]
    arrays = len(plan)
    others = refs[2 : 2 + arrays]
    at = 2 + arrays
    start = None
    if carry:
        start = refs[at]
        at += 1
    out, columns = refs[at], refs[at + 1]
    number = 0
    for ref, kinds in zip(others, plan):
        for index, kind in enumerate(kinds):
            block = ref[index] if len(ref.shape) == 3 else ref[...]
            times = multiplicity(kind, shift, groups, blocks)
            columns[number * count : (number + 1) * count, :] = block.T
            spot = slice(number * count, (number + 1) * count)
            columns[spot, 6:7] = columns[spot, 6:7] * times
            number += 1
    width = 2
    for half in range(count // (width * LANES)):
        spans = [slice((half * width + v) * LANES, (half * width + v + 1) * LANES) for v in range(width)]
        mine = [[jnp.broadcast_to(own[k : k + 1, s], (ROWS, LANES)) for k in range(6)] for s in spans]

        def body(step, sums):
            sums = [list(s) for s in sums]
            base = pl.multiple_of(step * ROWS, ROWS)
            group = columns[pl.ds(base, ROWS), :]
            b = [jnp.broadcast_to(group[:, k : k + 1], (ROWS, LANES)) for k in range(7)]
            for v in range(width):
                a, s = mine[v], sums[v]
                d0, d1, d2 = a[0] - b[0], a[1] - b[1], a[2] - b[2]
                dist = d0 * d0 + d1 * d1 + (d2 * d2 + EPS2)
                proj_a = a[3] * d0 + a[4] * d1 + a[5] * d2
                proj_b = b[3] * d0 + b[4] * d1 + b[5] * d2
                inverse = 1.0 / dist
                square = inverse * inverse * b[6]
                alpha = proj_a * square
                beta = proj_b * square
                kernel = proj_a * alpha + proj_b * beta
                gamma = 2.0 * (kernel * inverse)
                s[0] += beta * b[3] - gamma * d0
                s[1] += beta * b[4] - gamma * d1
                s[2] += beta * b[5] - gamma * d2
                s[3] += alpha * d0
                s[4] += alpha * d1
                s[5] += alpha * d2
                s[6] += alpha
                s[7] += kernel
            return tuple(tuple(s) for s in sums)

        zero = jnp.zeros((ROWS, LANES), F32)
        sums = lax.fori_loop(0, number * count // ROWS, body, ((zero,) * 8,) * width, unroll=2)
        for v, span in enumerate(spans):
            for k in range(8):
                row = jnp.sum(sums[v][k], axis=0, keepdims=True)
                if start is not None:
                    row = row + start[k : k + 1, span]
                out[k : k + 1, span] = row


def tiles(shift, own, parts, start, groups, blocks):
    arrays = [array for array, _ in parts]
    plan = tuple(kinds for _, kinds in parts)
    count = own.shape[1]
    number = sum(len(kinds) for kinds in plan)
    body = functools.partial(tiles_kernel, plan, groups, blocks, start is not None, 0)
    operands = [shift, own, *arrays] + ([start] if start is not None else [])
    pairs = number * count * count
    return pl.pallas_call(
        body,
        out_shape=jax.ShapeDtypeStruct((ROWS, count), F32),
        in_specs=[SMEM] + [VMEM] * (len(operands) - 1),
        out_specs=VMEM,
        scratch_shapes=[pltpu.VMEM((number * count, ROWS), F32)],
        cost_estimate=pl.CostEstimate(flops=60 * pairs, bytes_accessed=32 * count * number, transcendentals=pairs),
    )(*operands)


def finish_kernel(own, edges, sums, faces, grad, share):
    verts = grad.shape[1]
    count = own.shape[1]
    twice = 2.0 * own[6:7, :]
    total = sums[6:7, :]
    g_center = [twice * (own[3 + c : 4 + c, :] * total + sums[c : c + 1, :]) for c in range(3)]
    g_area = [twice * sums[3 + c : 4 + c, :] for c in range(3)]
    e1 = [edges[c : c + 1, :] for c in range(3)]
    e2 = [edges[3 + c : 4 + c, :] for c in range(3)]
    zero = jnp.zeros((ROWS - 3, count), F32)
    corners = [[], [], []]
    for c in range(3):
        n, m = (c + 1) % 3, (c + 2) % 3
        g1 = 0.5 * (e2[n] * g_area[m] - e2[m] * g_area[n])
        g2 = 0.5 * (g_area[n] * e1[m] - g_area[m] * e1[n])
        part = g_center[c] / 3.0
        corners[0].append(part - g1 - g2)
        corners[1].append(part + g1)
        corners[2].append(part + g2)
    total = jnp.zeros((3 * ROWS, verts), F32)
    for k in range(3):
        left = jnp.concatenate(pieces(jnp.concatenate(corners[k] + [zero], 0)), 0)
        total += lax.dot_general(
            left, one_hot(faces[k : k + 1, :], verts), (((1,), (1,)), ((), ())), preferred_element_type=F32
        )
    total = total[0:ROWS] + total[ROWS : 2 * ROWS] + total[2 * ROWS : 3 * ROWS]
    grad[...] = total[0:3] / count
    energy = own[6:7, :] * sums[7:8, :]
    share[...] = jnp.broadcast_to(0.5 * jnp.sum(energy, axis=1, keepdims=True), share.shape)


def shards(vertices, faces, trial_step, accepted, face_weight, partner_shift):
    count = faces.shape[1]
    verts = vertices.shape[1]
    groups, blocks = lax.axis_size("grp"), lax.axis_size("blk")
    block_shape = jax.ShapeDtypeStruct((ROWS, count), F32)
    own, edges = pl.pallas_call(
        geometry_kernel,
        out_shape=(block_shape, block_shape),
        in_specs=[SMEM] + [VMEM] * 4,
        out_specs=(VMEM, VMEM),
        scratch_shapes=[pltpu.VMEM((ROWS, verts), F32)],
    )(accepted, vertices, trial_step, faces, face_weight)
    visit = functools.partial(tiles, partner_shift, own, groups=groups, blocks=blocks)

    blk_parts, grp_parts = [], []
    held, kinds = own[None], [0]
    if blocks & (blocks - 1) == 0 and blocks <= 2 * HOPS:
        mask = blocks // 2
        while mask:
            other = flip(held, "blk", mask)
            kinds_other = [k ^ mask for k in kinds]
            blk_parts.append((other, tuple(("blk^", k) for k in kinds_other)))
            held, kinds = jnp.concatenate([held, other], 0), kinds + kinds_other
            mask //= 2
    else:
        offsets = sorted({o for k in range(1, HOPS + 1) for o in (k % blocks, -k % blocks) if o})
        for o in offsets:
            blk_parts.append((from_ahead(own, "blk", o), (("blk", o),)))
    held, kinds = own[None], [0]
    if groups & (groups - 1) == 0:
        mask = groups // 2
        while mask:
            other = flip(held, "grp", mask)
            kinds_other = [k ^ mask for k in kinds]
            grp_parts.append((other, tuple(("grp^", k) for k in kinds_other)))
            held, kinds = jnp.concatenate([held, other], 0), kinds + kinds_other
            mask //= 2
    else:
        for o in range(1, groups):
            grp_parts.append((from_ahead(own, "grp", o), (("grp", o),)))

    sums = visit([(own, (("self", 0),))], None)
    for i in range(max(len(blk_parts), len(grp_parts))):
        sums = visit(blk_parts[i : i + 1] + grp_parts[i : i + 1], sums)

    grad, share = pl.pallas_call(
        finish_kernel,
        out_shape=(jax.ShapeDtypeStruct((3, verts), F32), jax.ShapeDtypeStruct((ROWS, LANES), F32)),
        in_specs=[VMEM] * 4,
        out_specs=(VMEM, VMEM),
    )(own, edges, sums, faces)
    for axis, size in (("grp", groups), ("blk", blocks)):
        if size & (size - 1) == 0:
            mask = 1
            while mask < size:
                share = share + flip(share, axis, mask)
                mask *= 2
        else:
            share = share + sum(from_ahead(share, axis, o) for o in range(1, size))
    energy = share[0, 0:1] / (count * count * groups * blocks)
    return grad, energy


def solution(mesh):
    placed = (
        P(None, ("grp", "blk")),
        P(None, ("grp", "blk")),
        P(None, ("grp", "blk")),
        P("grp"),
        P(("grp", "blk")),
        P(),
    )
    return jax.shard_map(
        shards,
        mesh=mesh,
        in_specs=placed,
        out_specs=(P(None, ("grp", "blk")), P()),
        check_vma=False,
    )
```

time: 133 us -> 122 us (0.917)
  Pallas kernels: 0 us -> 84.2 us
  blocking collectives: 44.3 us -> 0 us
  other arithmetic: 38.9 us -> 1.43 us
  between operations: 22.6 us -> 3.08 us
  waiting for transfers between devices: 1.55 us -> 15.8 us
  local copies, waits for them, and re-layouts: 7.44 us -> 2.37 us
  starting transfers between devices: 17.5 us -> 14.4 us
    pallas_call x0 -> x6, Pallas kernels: none -> 84.2 us  [the longest x4 80.9 us: tiles(): pl.pallas_call(body, out_shape=jax.ShapeDtypeStruct((ROWS, count), F32),...]
    psum x1 -> x0, blocking collectives: 39.1 us -> none  [shards(): total = lax.psum(energy, ('grp', 'blk'))]
    reduce_sum x6 -> x0, other arithmetic: 29 us -> none  [pair_energy(): return jnp.sum(kernel)]
    ppermute x10, waiting for transfers between devices: 1.51 us -> 15.8 us  [flip(): return lax.ppermute(value, axis, [(i, i ^ mask) for i in range(count)])]
    scatter-add x3 -> x0, other arithmetic: 7.94 us -> none  [the longest x1 3.37 us: geometry(): first = pos[:, faces[0]]]
    all_gather x1 -> x0, blocking collectives: 5.24 us -> none  [shards(): blocks = lax.all_gather(own[None], 'grp', axis=0, tiled=True)]
    gather x6 -> x0, local copies, waits for them, and re-layouts: 3.44 us -> none  [the longest x2 1.15 us: geometry(): first = pos[:, faces[0]]]
    ppermute x10, starting transfers between devices: 17.4 us -> 14.4 us  [flip(): return lax.ppermute(value, axis, [(i, i ^ mask) for i in range(count)])]
  transfers between devices with their start and end apart: 11 -> 10, of which waited for: 1 -> 7; matrix products, arithmetic and copies ran while one was open for 23% -> 0% of each run, Pallas kernels for 0% -> 43%
where the time goes in v1:
time: 122 us; the launch traced here: 121 us
  Pallas kernels  84.2 us (69%)
  waiting for transfers between devices  15.8 us (13%)
  starting transfers between devices  14.4 us (12%)
  between operations  3.08 us (3%)
  local copies, waits for them, and re-layouts  2.37 us (2%)
  other arithmetic  1.43 us (1%)
    pallas_call x4, Pallas kernels, tiles(): pl.pallas_call(body, out_shape=jax.ShapeDtypeStruct((ROWS, count), F32),...  80.9 us
    ppermute x10, waiting for transfers between devices, flip(): return lax.ppermute(value, axis, [(i, i ^ mask) for i in range(count)])  15.8 us
    ppermute x10, starting transfers between devices, flip(): return lax.ppermute(value, axis, [(i, i ^ mask) for i in range(count)])  14.4 us
  transfers between devices with their start and end apart: 10, of which 7 were waited for; matrix products, arithmetic and copies ran while one was open for 0% of the time, Pallas kernels for 43%

profile of v1, /device:TPU:0, one launch (start us, length us, event | category | flops | bytes accessed | tf_op | source)
XLA Modules:
  0.0 121.2 jit_solution(5456744443541550704)
XLA Ops:
  1.3 1.6 %shard_map.77 = (f32[8,512]{1,0:T(8,128)}, f32[8,512]{1,0:T(8,128)}) custom-call(s32[1]{0:T(128)S(6)} %copy.8.accepted, f32[3,256]{1,0:T(4,128)} %vertices.1, f32[3,256]{1,0:T(4,128)} %trial_step.1, s32[3,512]{1,0:T(4,128)} %faces.3, f32[512]{0:T(512)} %weight.1), custom_call_target="tpu_custom_call" | custom-call | tf_op jit(solution)/shard_map/pallas_call | solution.py:217
  2.9 0.0 copy-start
  2.9 3.0 %collective-permute-start.3 = (f32[1,8,512]{2,1,0:T(8,128)}, f32[1,8,512]{2,1,0:T(8,128)S(1)}, u32[]{:S(2)}, u32[]{:S(2)}) collective-permute-start(f32[1,8,512]{2,1,0:T(8,128)} %bitcast.2), channel_id=1, source_target_pairs={{0,16},{8,24},{16,0},{24,8},{1,17},{9,25},{17,1},{25,9},{2,18},{10... | collective-permute-start | bytes 49160 | tf_op jit(solution)/shard_map/ppermute | solution.py:22
  5.8 2.6 %collective-permute-start = (f32[1,8,512]{2,1,0:T(8,128)}, f32[1,8,512]{2,1,0:T(8,128)S(1)}, u32[]{:S(2)}, u32[]{:S(2)}) collective-permute-start(f32[1,8,512]{2,1,0:T(8,128)} %bitcast.3), channel_id=1, source_target_pairs={{0,4},{1,5},{2,6},{3,7},{4,0},{5,1},{6,2},{7,3},{8,12},{9,13},{10,... | collective-permute-start | bytes 49160 | tf_op jit(solution)/shard_map/ppermute | solution.py:22
  8.4 0.0 collective-permute-done.3.refs_3_
  8.4 0.0 copy-start.3
  8.4 2.3 %collective-permute-done.refs_2_ = f32[1,8,512]{2,1,0:T(8,128)S(1)} collective-permute-done((f32[1,8,512]{2,1,0:T(8,128)}, f32[1,8,512]{2,1,0:T(8,128)S(1)}, u32[]{:S(2)}, u32[]{:S(2)}) %collective-permute-start) | collective-permute-done | bytes 16416 | tf_op jit(solution)/shard_map/ppermute | solution.py:22
  10.7 0.0 copy-start.1
  10.7 0.7 pad_maximum_fusion.1
  11.4 0.0 copy-done.3
  11.4 1.6 %collective-permute-start.1 = (f32[2,8,512]{2,1,0:T(8,128)S(1)}, f32[2,8,512]{2,1,0:T(8,128)S(1)}, u32[]{:S(2)}, u32[]{:S(2)}) collective-permute-start(f32[2,8,512]{2,1,0:T(8,128)S(1)} %get-tuple-element.11), channel_id=1, source_target_pairs={{0,2},{1,3},{2,0},{3,1},{4,6},{5,7},{6,4},{7,5},{8,10},{9,11},{10,... | collective-permute-start | bytes 98312 | tf_op jit(solution)/shard_map/ppermute | solution.py:22
  13.0 2.3 %collective-permute-done.1.refs_2_ = f32[2,8,512]{2,1,0:T(8,128)S(1)} collective-permute-done((f32[2,8,512]{2,1,0:T(8,128)S(1)}, f32[2,8,512]{2,1,0:T(8,128)S(1)}, u32[]{:S(2)}, u32[]{:S(2)}) %collective-permute-start.1) | collective-permute-done | bytes 32800 | tf_op jit(solution)/shard_map/ppermute | solution.py:22
  15.3 0.0 copy-done.1
  15.3 0.0 copy-done
  15.4 0.0 copy-start.2
  15.4 0.6 copy-done.2
  16.0 1.5 %collective-permute-start.2 = (f32[4,8,512]{2,1,0:T(8,128)S(1)}, f32[4,8,512]{2,1,0:T(8,128)S(1)}, u32[]{:S(2)}, u32[]{:S(2)}) collective-permute-start(f32[4,8,512]{2,1,0:T(8,128)S(1)} %pad_maximum_fusion), channel_id=1, source_target_pairs={{0,1},{1,0},{2,3},{3,2},{4,5},{5,4},{6,7},{7,6},{8,9},{9,8},{10,11... | collective-permute-start | bytes 196616 | tf_op jit(solution)/shard_map/ppermute | solution.py:22
  17.5 0.0 collective-permute-start.4
  17.5 8.3 %shard_map.78.refs_4_ = f32[8,512]{1,0:T(8,128)} custom-call(s32[2,4]{1,0:T(2,128)} %refs_0_.7, f32[8,512]{1,0:T(8,128)} %get-tuple-element.6.refs_1_.refs_2_.own, f32[8,512]{1,0:T(8,128)} %get-tuple-element.6.refs_1_.refs_2_.own), custom_call_target="tpu_custom_call" | custom-call | flops 15728640 | bytes 16384 | tf_op jit(solution)/shard_map/pallas_call | solution.py:171
  25.8 15.1 %shard_map.79.refs_4_ = f32[8,512]{1,0:T(8,128)} custom-call(s32[2,4]{1,0:T(2,128)} %refs_0_.7, f32[8,512]{1,0:T(8,128)} %get-tuple-element.6.refs_1_.refs_2_.own, f32[1,8,512]{2,1,0:T(8,128)} %copy-done.1, f32[1,8,512]{2,1,0:T(8,128)} %copy-done.3, f32[8,512]{1,0:T(8,128)} %shard_map.78.refs_4_), custom_call_target="tpu_custom_call" | custom-call | flops 31457280 | bytes 32768 | tf_op jit(solution)/shard_map/pallas_call | solution.py:171
  40.9 0.0 collective-permute-done.4.refs_3_
  40.9 0.0 copy-start.5
  40.9 0.6 copy-done.5
  41.5 28.7 %shard_map.80.refs_3_ = f32[8,512]{1,0:T(8,128)} custom-call(s32[2,4]{1,0:T(2,128)} %refs_0_.7, f32[8,512]{1,0:T(8,128)} %get-tuple-element.6.refs_1_.refs_2_.own, f32[2,8,512]{2,1,0:T(8,128)} %copy-done.2, f32[2,8,512]{2,1,0:T(8,128)} %copy-done.5, f32[8,512]{1,0:T(8,128)} %shard_map.79.refs_4_), custom_call_target="tpu_custom_call" | custom-call | flops 62914560 | bytes 65536 | tf_op jit(solution)/shard_map/pallas_call | solution.py:171
  70.3 0.0 collective-permute-done.2.refs_2_
  70.3 0.0 copy-start.4
  70.3 0.6 copy-done.4
  70.9 28.7 %shard_map.81.sums = f32[8,512]{1,0:T(8,128)} custom-call(s32[2,4]{1,0:T(2,128)} %refs_0_.7, f32[8,512]{1,0:T(8,128)} %get-tuple-element.6.refs_1_.refs_2_.own, f32[4,8,512]{2,1,0:T(8,128)} %copy-done.4, f32[8,512]{1,0:T(8,128)} %shard_map.80.refs_3_), custom_call_target="tpu_custom_call" | custom-call | flops 62914560 | bytes 65536 | tf_op jit(solution)/shard_map/pallas_call | solution.py:171
  99.6 1.7 %shard_map.82 = (f32[3,256]{1,0:T(4,128)}, f32[8,128]{1,0:T(8,128)}) custom-call(f32[8,512]{1,0:T(8,128)} %get-tuple-element.6.refs_1_.refs_2_.own, f32[8,512]{1,0:T(8,128)} %get-tuple-element.7.edges, f32[8,512]{1,0:T(8,128)} %shard_map.81.sums, s32[3,512]{1,0:T(4,128)} %faces.3), custom_call_target="tpu_custom_call" | custom-call | tf_op jit(solution)/shard_map/pallas_call | solution.py:257
  101.3 0.5 collective-permute-start.5
  101.8 1.0 collective-permute-done.5
  102.9 0.7 add.15
  103.6 0.5 collective-permute-start.6
  104.1 3.1 %collective-permute-done.6 = f32[8,128]{1,0:T(8,128)S(1)} collective-permute-done((f32[8,128]{1,0:T(8,128)S(1)}, f32[8,128]{1,0:T(8,128)S(1)}, u32[]{:S(2)}, u32[]{:S(2)}) %collective-permute-start.6) | collective-permute-done | bytes 4128 | tf_op jit(solution)/shard_map/ppermute | solution.py:22
  107.2 0.5 collective-permute-start.7
  107.7 3.1 %collective-permute-done.7 = f32[8,128]{1,0:T(8,128)S(1)} collective-permute-done((f32[8,128]{1,0:T(8,128)S(1)}, f32[8,128]{1,0:T(8,128)S(1)}, u32[]{:S(2)}, u32[]{:S(2)}) %collective-permute-start.7) | collective-permute-done | bytes 4128 | tf_op jit(solution)/shard_map/ppermute | solution.py:22
  110.8 1.6 %collective-permute-start.8 = (f32[8,128]{1,0:T(8,128)S(1)}, f32[8,128]{1,0:T(8,128)S(1)}, u32[]{:S(2)}, u32[]{:S(2)}) collective-permute-start(f32[8,128]{1,0:T(8,128)S(1)} %add.17), channel_id=1, source_target_pairs={{0,2},{1,3},{2,0},{3,1},{4,6},{5,7},{6,4},{7,5},{8,10},{9,11},{10,... | collective-permute-start | bytes 12296 | tf_op jit(solution)/shard_map/ppermute | solution.py:22
  112.3 2.0 %collective-permute-done.8 = f32[8,128]{1,0:T(8,128)S(1)} collective-permute-done((f32[8,128]{1,0:T(8,128)S(1)}, f32[8,128]{1,0:T(8,128)S(1)}, u32[]{:S(2)}, u32[]{:S(2)}) %collective-permute-start.8) | collective-permute-done | bytes 4128 | tf_op jit(solution)/shard_map/ppermute | solution.py:22
  114.4 2.6 %collective-permute-start.9 = (f32[8,128]{1,0:T(8,128)S(1)}, f32[8,128]{1,0:T(8,128)S(1)}, u32[]{:S(2)}, u32[]{:S(2)}) collective-permute-start(f32[8,128]{1,0:T(8,128)S(1)} %add.18), channel_id=1, source_target_pairs={{0,4},{1,5},{2,6},{3,7},{4,0},{5,1},{6,2},{7,3},{8,12},{9,13},{10,... | collective-permute-start | bytes 12296 | tf_op jit(solution)/shard_map/ppermute | solution.py:22
  117.0 1.9 %collective-permute-done.9 = f32[8,128]{1,0:T(8,128)S(1)} collective-permute-done((f32[8,128]{1,0:T(8,128)S(1)}, f32[8,128]{1,0:T(8,128)S(1)}, u32[]{:S(2)}, u32[]{:S(2)}) %collective-permute-start.9) | collective-permute-done | bytes 4128 | tf_op jit(solution)/shard_map/ppermute | solution.py:22
  118.9 0.5 slice.3
  (5 shorter events, 0.0 us)
Async XLA Ops:
  2.9 12.5 %copy-start = (f32[8,512]{1,0:T(8,128)S(1)}, f32[8,512]{1,0:T(8,128)}, u32[]{:S(2)}) copy-start(f32[8,512]{1,0:T(8,128)} %get-tuple-element.6.refs_1_.refs_2_.own) | copy-start | bytes 49156
  2.9 5.6 %collective-permute-start.3 = (f32[1,8,512]{2,1,0:T(8,128)}, f32[1,8,512]{2,1,0:T(8,128)S(1)}, u32[]{:S(2)}, u32[]{:S(2)}) collective-permute-start(f32[1,8,512]{2,1,0:T(8,128)} %bitcast.2), channel_id=1, source_target_pairs={{0,16},{8,24},{16,0},{24,8},{1,17},{9,25},{17,1},{25,9},{2,18},{10... | collective-permute-start | bytes 49160 | tf_op jit(solution)/shard_map/ppermute | solution.py:22
  5.8 4.8 %collective-permute-start = (f32[1,8,512]{2,1,0:T(8,128)}, f32[1,8,512]{2,1,0:T(8,128)S(1)}, u32[]{:S(2)}, u32[]{:S(2)}) collective-permute-start(f32[1,8,512]{2,1,0:T(8,128)} %bitcast.3), channel_id=1, source_target_pairs={{0,4},{1,5},{2,6},{3,7},{4,0},{5,1},{6,2},{7,3},{8,12},{9,13},{10,... | collective-permute-start | bytes 49160 | tf_op jit(solution)/shard_map/ppermute | solution.py:22
  8.4 3.0 %copy-start.3 = (f32[1,8,512]{2,1,0:T(8,128)}, f32[1,8,512]{2,1,0:T(8,128)S(1)}, u32[]{:S(2)}) copy-start(f32[1,8,512]{2,1,0:T(8,128)S(1)} %collective-permute-done.3.refs_3_) | copy-start | bytes 49156
  10.7 4.7 %copy-start.1 = (f32[1,8,512]{2,1,0:T(8,128)}, f32[1,8,512]{2,1,0:T(8,128)S(1)}, u32[]{:S(2)}) copy-start(f32[1,8,512]{2,1,0:T(8,128)S(1)} %collective-permute-done.refs_2_) | copy-start | bytes 49156
  11.4 3.9 %collective-permute-start.1 = (f32[2,8,512]{2,1,0:T(8,128)S(1)}, f32[2,8,512]{2,1,0:T(8,128)S(1)}, u32[]{:S(2)}, u32[]{:S(2)}) collective-permute-start(f32[2,8,512]{2,1,0:T(8,128)S(1)} %get-tuple-element.11), channel_id=1, source_target_pairs={{0,2},{1,3},{2,0},{3,1},{4,6},{5,7},{6,4},{7,5},{8,10},{9,11},{10,... | collective-permute-start | bytes 98312 | tf_op jit(solution)/shard_map/ppermute | solution.py:22
  15.4 0.6 copy-start.2
  16.0 54.3 %collective-permute-start.2 = (f32[4,8,512]{2,1,0:T(8,128)S(1)}, f32[4,8,512]{2,1,0:T(8,128)S(1)}, u32[]{:S(2)}, u32[]{:S(2)}) collective-permute-start(f32[4,8,512]{2,1,0:T(8,128)S(1)} %pad_maximum_fusion), channel_id=1, source_target_pairs={{0,1},{1,0},{2,3},{3,2},{4,5},{5,4},{6,7},{7,6},{8,9},{9,8},{10,11... | collective-permute-start | bytes 196616 | tf_op jit(solution)/shard_map/ppermute | solution.py:22
  17.5 23.4 %collective-permute-start.4 = (f32[2,8,512]{2,1,0:T(8,128)S(1)}, f32[2,8,512]{2,1,0:T(8,128)S(1)}, u32[]{:S(2)}, u32[]{:S(2)}) collective-permute-start(f32[2,8,512]{2,1,0:T(8,128)S(1)} %get-tuple-element.10), channel_id=1, source_target_pairs={{0,8},{8,0},{16,24},{24,16},{1,9},{9,1},{17,25},{25,17},{2,10},{10... | collective-permute-start | bytes 98312 | tf_op jit(solution)/shard_map/ppermute | solution.py:22
  40.9 0.6 copy-start.5
  70.3 0.6 copy-start.4
  101.3 1.5 %collective-permute-start.5 = (f32[8,128]{1,0:T(8,128)}, f32[8,128]{1,0:T(8,128)S(1)}, u32[]{:S(2)}, u32[]{:S(2)}) collective-permute-start(f32[8,128]{1,0:T(8,128)} %get-tuple-element.9), channel_id=1, source_target_pairs={{0,8},{8,0},{16,24},{24,16},{1,9},{9,1},{17,25},{25,17},{2,10},{10... | collective-permute-start | bytes 12296 | tf_op jit(solution)/shard_map/ppermute | solution.py:22
  103.6 3.6 %collective-permute-start.6 = (f32[8,128]{1,0:T(8,128)S(1)}, f32[8,128]{1,0:T(8,128)S(1)}, u32[]{:S(2)}, u32[]{:S(2)}) collective-permute-start(f32[8,128]{1,0:T(8,128)S(1)} %add.15), channel_id=1, source_target_pairs={{0,16},{8,24},{16,0},{24,8},{1,17},{9,25},{17,1},{25,9},{2,18},{10... | collective-permute-start | bytes 12296 | tf_op jit(solution)/shard_map/ppermute | solution.py:22
  107.2 3.6 %collective-permute-start.7 = (f32[8,128]{1,0:T(8,128)S(1)}, f32[8,128]{1,0:T(8,128)S(1)}, u32[]{:S(2)}, u32[]{:S(2)}) collective-permute-start(f32[8,128]{1,0:T(8,128)S(1)} %add.16), channel_id=1, source_target_pairs={{0,1},{1,0},{2,3},{3,2},{4,5},{5,4},{6,7},{7,6},{8,9},{9,8},{10,11... | collective-permute-start | bytes 12296 | tf_op jit(solution)/shard_map/ppermute | solution.py:22
  110.8 3.6 %collective-permute-start.8 = (f32[8,128]{1,0:T(8,128)S(1)}, f32[8,128]{1,0:T(8,128)S(1)}, u32[]{:S(2)}, u32[]{:S(2)}) collective-permute-start(f32[8,128]{1,0:T(8,128)S(1)} %add.17), channel_id=1, source_target_pairs={{0,2},{1,3},{2,0},{3,1},{4,6},{5,7},{6,4},{7,5},{8,10},{9,11},{10,... | collective-permute-start | bytes 12296 | tf_op jit(solution)/shard_map/ppermute | solution.py:22
  114.4 4.5 %collective-permute-start.9 = (f32[8,128]{1,0:T(8,128)S(1)}, f32[8,128]{1,0:T(8,128)S(1)}, u32[]{:S(2)}, u32[]{:S(2)}) collective-permute-start(f32[8,128]{1,0:T(8,128)S(1)} %add.18), channel_id=1, source_target_pairs={{0,4},{1,5},{2,6},{3,7},{4,0},{5,1},{6,2},{7,3},{8,12},{9,13},{10,... | collective-permute-start | bytes 12296 | tf_op jit(solution)/shard_map/ppermute | solution.py:22
